TPU v7x, 256 devices: a whole 4x4x8 slice. The times are simulated.
256 devices in a mesh: segment: 4 (over x), shard: 64 (over y, z, core).
Axes of the slice: x: 4, y: 4, z: 8, core: 2. Of those that a mesh axis runs over, the one named last changes fastest.
Arguments:
- tokens: bfloat16 [3, 128, 3072], P(None, 'shard'), may hold values from -6 to 6
- norm_gain: float32 [4, 3072], P('segment'), may hold values from 0.5 to 1.5
- w_gate: bfloat16 [4, 3072, 32768], P('segment', None, 'shard'), may hold values from -0.109375 to 0.109375
- w_up: bfloat16 [4, 3072, 32768], P('segment', None, 'shard'), may hold values from -0.109375 to 0.109375
- w_down: bfloat16 [4, 32768, 3072], P('segment', 'shard'), may hold values from -0.046875 to 0.046875
- block_counts: int32 [4], P('segment'), may hold values from 1 to 2
- gate_prob: float32 [4, 3, 128], P('segment', None, 'shard'), may hold values from 0.1 to 1
Outputs:
- section_outputs: bfloat16 [4, 3, 128, 3072], P('segment', None, 'shard')
All inputs are finite; a program needn't handle non-finite values.
Results may differ from a plain program's by a relative error of at most 0.009.
Values may be sent and summed in bfloat16 or wider, within the bound.
A program may use at most 64 MiB of HBM per device.

v0:
```python
import jax
import jax.numpy as jnp
from jax import lax
from jax.sharding import PartitionSpec as P

FF = 16384


def shifted(value, axis, steps):
    count = lax.axis_size(axis)
    initial, last = (max(0, -steps), min(count, count - steps))
    return lax.ppermute(value, axis, [(source, source + steps) for source in range(initial, last)])


def normalize(rows, row_gain):
    values = rows.astype(jnp.float32)
    scale = lax.rsqrt(jnp.mean(values * values, axis=-1, keepdims=True) + 1e-05)
    return (values * scale * row_gain).astype(jnp.bfloat16)


def expert_rows(normed, gate_part, up_part, down_part):
    gate_val = jnp.dot(normed, gate_part, preferred_element_type=jnp.float32)
    up_val = jnp.dot(normed, up_part, preferred_element_type=jnp.float32)
    hidden = (jax.nn.silu(gate_val) * up_val).astype(jnp.bfloat16)
    return jnp.dot(hidden, down_part, preferred_element_type=jnp.float32)


def shards(tokens, norm_gain, w_gate, w_up, w_down, block_counts, gate_prob):
    segment_index = lax.axis_index("segment")
    segment_count = lax.axis_size("segment")
    shard_count = lax.axis_size("shard")
    hidden_count = w_gate.shape[2]
    own_expert = lax.axis_index("shard") // (FF // hidden_count)
    zero_blocks = block_counts[0]
    row_gain = norm_gain[0]
    gate_part = w_gate[0]
    up_part = w_up[0]
    down_part = w_down[0]
    probs = gate_prob[0]
    block_total = tokens.shape[0]
    local_rows = tokens.shape[1]
    width = tokens.shape[2]
    first_block = jnp.where(own_expert == 0, 0, zero_blocks)
    last_block = jnp.where(own_expert == 0, zero_blocks, block_total)
    carried = tokens
    stored = jnp.zeros_like(tokens)
    for tick in range(segment_count):
        normed = normalize(carried, row_gain)
        gathered = lax.all_gather(normed, "shard", axis=1, tiled=True)
        partial_sum = jnp.zeros(gathered.shape, jnp.float32)

        def add_block(block_id, acc):
            block_rows = lax.dynamic_index_in_dim(gathered, block_id, 0, keepdims=False)
            result = expert_rows(block_rows, gate_part, up_part, down_part)
            return lax.dynamic_update_index_in_dim(acc, result, block_id, 0)

        partial_sum = lax.fori_loop(first_block, last_block, add_block, partial_sum)
        split_terms = partial_sum.reshape(block_total, shard_count, local_rows, width)
        received = lax.all_to_all(split_terms, "shard", split_axis=1, concat_axis=1, tiled=True)
        mixed = jnp.sum(received, axis=1)
        updated = (carried.astype(jnp.float32) + probs[:, :, None] * mixed).astype(jnp.bfloat16)
        stored = jnp.where(segment_index == tick, updated, stored)
        if tick + 1 < segment_count:
            carried = shifted(updated, "segment", 1)
    return stored[None]


def solution(mesh):
    placed = (
        P(None, "shard", None),
        P("segment", None),
        P("segment", None, "shard"),
        P("segment", None, "shard"),
        P("segment", "shard", None),
        P("segment"),
        P("segment", None, "shard"),
    )
    return jax.shard_map(
        shards,
        mesh=mesh,
        in_specs=placed,
        out_specs=P("segment", None, "shard", None),
        check_vma=False,
    )
```

profile of v0, /device:TPU:5, one launch (start us, length us, event | category | flops | bytes accessed | tf_op | source)
XLA Modules:
  0.0 946.9 jit_solution(11908347532508689451)
XLA Ops:
  9.6 82.2 %all-gather.5.cloned.1.call-done = bf16[3,128,3072]{2,0,1:T(4,128)(2,1)} async-done(((bf16[3,2,3072]{2,0,1:T(4,128)(2,1)}), bf16[3,128,3072]{2,0,1:T(4,128)(2,1)}) %all-gather.5.cloned.1.call-update) | async-done | bytes 2359312 | tf_op jit(solution)/shard_map/all_gather | solution.py:49
  91.9 4.2 copy.27
  96.1 2.7 broadcast.59.clone
  98.9 7.1 while.40
  98.9 1.7 fusion.138
  100.6 5.4 fusion.139
  106.0 6.6 reshape.46
  112.6 6.1 copy.28
  118.6 13.8 %all-to-all-start = ((f32[3,64,2,3072]{3,2,0,1:T(2,128)}), f32[3,64,2,3072]{3,2,0,1:T(2,128)}, u32[]{:S(2)}, u32[]{:S(2)}) async-start(f32[3,64,2,3072]{3,2,0,1:T(2,128)} %copy.28), calls=%async_computation | async-start | bytes 9437184 | tf_op jit(solution)/shard_map/all_to_all | solution.py:59
  132.6 107.0 %all-to-all-done = f32[3,64,2,3072]{3,2,0,1:T(2,128)} async-done(((f32[3,64,2,3072]{3,2,0,1:T(2,128)}), f32[3,64,2,3072]{3,2,0,1:T(2,128)}, u32[]{:S(2)}, u32[]{:S(2)}) %all-to-all-start) | async-done | bytes 4718624 | tf_op jit(solution)/shard_map/all_to_all | solution.py:59
  239.6 3.7 reduce_sum.73
  243.3 2.8 collective-permute-start
  246.2 1.9 collective-permute-done
  249.0 76.5 %all-gather.7.cloned.1.call-done = bf16[3,128,3072]{2,0,1:T(4,128)(2,1)} async-done(((bf16[3,2,3072]{2,0,1:T(4,128)(2,1)}), bf16[3,128,3072]{2,0,1:T(4,128)(2,1)}) %all-gather.7.cloned.1.call-update) | async-done | bytes 2359312 | tf_op jit(solution)/shard_map/all_gather | solution.py:49
  325.5 4.2 copy.30
  329.7 2.7 broadcast.59.clone.1
  332.4 7.1 while.41
  332.4 1.7 fusion.145
  334.2 5.4 fusion.146
  339.5 6.6 reshape.47
  346.1 4.0 copy.31
  350.1 120.6 %all_to_all.20 = f32[3,64,2,3072]{3,2,0,1:T(2,128)} all-to-all(f32[3,64,2,3072]{3,2,0,1:T(2,128)S(1)} %copy.31), channel_id=1, replica_groups=mesh['segment'=4,'shard'=64] {'shard'}, dimensions={1} | all-to-all | bytes 9437184 | tf_op jit(solution)/shard_map/all_to_all | solution.py:59
  470.6 3.7 reduce_sum.75
  474.4 2.8 collective-permute-start.1
  477.2 1.9 collective-permute-done.1
  480.1 76.9 %all-gather.9.cloned.1.call-done = bf16[3,128,3072]{2,0,1:T(4,128)(2,1)} async-done(((bf16[3,2,3072]{2,0,1:T(4,128)(2,1)}), bf16[3,128,3072]{2,0,1:T(4,128)(2,1)}) %all-gather.9.cloned.1.call-update) | async-done | bytes 2359312 | tf_op jit(solution)/shard_map/all_gather | solution.py:49
  557.0 4.2 copy.33
  561.2 2.7 broadcast.59.clone.2
  563.9 7.1 while.42
  563.9 1.7 fusion.152
  565.6 5.4 fusion.153
  571.0 6.6 reshape.48
  577.6 4.0 copy.34
  581.6 120.6 %all_to_all.21 = f32[3,64,2,3072]{3,2,0,1:T(2,128)} all-to-all(f32[3,64,2,3072]{3,2,0,1:T(2,128)S(1)} %copy.34), channel_id=1, replica_groups=mesh['segment'=4,'shard'=64] {'shard'}, dimensions={1} | all-to-all | bytes 9437184 | tf_op jit(solution)/shard_map/all_to_all | solution.py:59
  702.1 3.7 reduce_sum.77
  705.9 2.8 collective-permute-start.2
  708.7 1.9 collective-permute-done.2
  711.5 77.0 %all-gather.11.cloned.1.call-done = bf16[3,128,3072]{2,0,1:T(4,128)(2,1)} async-done(((bf16[3,2,3072]{2,0,1:T(4,128)(2,1)}), bf16[3,128,3072]{2,0,1:T(4,128)(2,1)}) %all-gather.11.cloned.1.call-update) | async-done | bytes 2359312 | tf_op jit(solution)/shard_map/all_gather | solution.py:49
  788.5 4.2 copy.36
  792.7 2.7 broadcast.59
  795.4 7.1 while.43
  795.4 1.7 fusion.159
  797.2 5.4 fusion.160
  802.5 6.6 reshape.49
  809.1 6.1 copy.37
  815.2 13.7 %all-to-all-start.3 = ((f32[3,64,2,3072]{3,2,0,1:T(2,128)}), f32[3,64,2,3072]{3,2,0,1:T(2,128)}, u32[]{:S(2)}, u32[]{:S(2)}) async-start(f32[3,64,2,3072]{3,2,0,1:T(2,128)} %copy.37), calls=%async_computation.3 | async-start | bytes 9437184 | tf_op jit(solution)/shard_map/all_to_all | solution.py:59
  828.9 107.1 %all-to-all-done.3 = f32[3,64,2,3072]{3,2,0,1:T(2,128)} async-done(((f32[3,64,2,3072]{3,2,0,1:T(2,128)}), f32[3,64,2,3072]{3,2,0,1:T(2,128)}, u32[]{:S(2)}, u32[]{:S(2)}) %all-to-all-start.3) | async-done | bytes 4718624 | tf_op jit(solution)/shard_map/all_to_all | solution.py:59
  936.0 3.7 reduce_sum.79
  (41 shorter events, 6.5 us)
Async XLA Ops:
  6.5 85.3 %all-gather.5.cloned.1.call-start = ((), (), s32[]{:S(2)}) async-start(), calls=%async_computation.4 | async-start | bytes 3194880 | tf_op jit(solution)/shard_map/all_gather | solution.py:49
  96.1 2.8 copy-start
  118.6 13.9 %copy-start.5 = (f32[1,3,2]{1,2,0:T(2,128)S(1)}, f32[1,3,2]{1,2,0:T(2,128)}, u32[]{:S(2)}) copy-start(f32[1,3,2]{1,2,0:T(2,128)} %param.21) | copy-start | bytes 76
  118.6 120.9 %all-to-all-start = ((f32[3,64,2,3072]{3,2,0,1:T(2,128)}), f32[3,64,2,3072]{3,2,0,1:T(2,128)}, u32[]{:S(2)}, u32[]{:S(2)}) async-start(f32[3,64,2,3072]{3,2,0,1:T(2,128)} %copy.28), calls=%async_computation | async-start | bytes 9437184 | tf_op jit(solution)/shard_map/all_to_all | solution.py:59
  132.4 110.8 %copy-start.1 = (bf16[3,2,3072]{2,1,0:T(2,128)(2,1)S(1)}, bf16[3,2,3072]{2,1,0:T(2,128)(2,1)}, u32[]{:S(2)}) copy-start(bf16[3,2,3072]{2,1,0:T(2,128)(2,1)} %param.15) | copy-start | bytes 110596
  132.4 115.8 %copy-start.2 = (f32[1,3072]{1,0:T(1,128)S(1)}, f32[1,3072]{1,0:T(1,128)}, u32[]{:S(2)}) copy-start(f32[1,3072]{1,0:T(1,128)} %param.16) | copy-start | bytes 36868
  132.4 193.1 %all-gather.7.cloned.1.call-start = ((), (), s32[]{:S(2)}) async-start(), calls=%async_computation.5 | async-start | bytes 3194880 | tf_op jit(solution)/shard_map/all_gather | solution.py:49
  243.3 4.7 collective-permute-start
  249.0 308.0 %all-gather.9.cloned.1.call-start = ((), (), s32[]{:S(2)}) async-start(), calls=%async_computation.6 | async-start | bytes 3194880 | tf_op jit(solution)/shard_map/all_gather | solution.py:49
  474.4 4.7 collective-permute-start.1
  480.0 308.5 %all-gather.11.cloned.1.call-start = ((), (), s32[]{:S(2)}) async-start(), calls=%async_computation.7 | async-start | bytes 3194880 | tf_op jit(solution)/shard_map/all_gather | solution.py:49
  705.9 89.5 %copy-start.3 = (bf16[3,2,3072]{2,1,0:T(2,128)(2,1)}, bf16[3,2,3072]{2,1,0:T(2,128)(2,1)S(1)}, u32[]{:S(2)}) copy-start(bf16[3,2,3072]{2,1,0:T(2,128)(2,1)S(1)} %fusion.87) | copy-start | bytes 110596
  705.9 4.7 collective-permute-start.2
  815.2 120.8 %all-to-all-start.3 = ((f32[3,64,2,3072]{3,2,0,1:T(2,128)}), f32[3,64,2,3072]{3,2,0,1:T(2,128)}, u32[]{:S(2)}, u32[]{:S(2)}) async-start(f32[3,64,2,3072]{3,2,0,1:T(2,128)} %copy.37), calls=%async_computation.3 | async-start | bytes 9437184 | tf_op jit(solution)/shard_map/all_to_all | solution.py:59
  828.8 110.8 %copy-start.4 = (bf16[3,2,3072]{2,1,0:T(2,128)(2,1)S(1)}, bf16[3,2,3072]{2,1,0:T(2,128)(2,1)}, u32[]{:S(2)}) copy-start(bf16[3,2,3072]{2,1,0:T(2,128)(2,1)} %copy-done.3) | copy-start | bytes 110596
Sparse Core Ops, SparseCore 0:
  10.1 81.7 all-gather.4
  249.1 76.3 all-gather.6
  480.1 76.8 all-gather.8
  711.6 76.8 all-gather.10
where the time goes:
time: 949 us; the launch traced here: 947 us
  waiting for transfers between devices  532 us (56%)
  blocking collectives  241 us (25%)
  local copies, waits for them, and re-layouts  76.8 us (8%)
  starting transfers between devices  36 us (4%)
  matrix products  28.3 us (3%)
  other arithmetic  18.2 us (2%)
  between operations  14 us (1%)
    all_gather x4, waiting for transfers between devices, shards(): gathered = lax.all_gather(normed, 'shard', axis=1, tiled=True)  313 us
    all_to_all x2, blocking collectives, shards(): lax.all_to_all(split_terms, 'shard', split_axis=1, concat_axis=1, tiled=T...  241 us
    all_to_all x2, waiting for transfers between devices, shards(): lax.all_to_all(split_terms, 'shard', split_axis=1, concat_axis=1, tiled=T...  214 us
    reshape x8, local copies, waits for them, and re-layouts, shards(): partial_sum.reshape(block_total, shard_count, local_rows, width)  46.4 us
    all_to_all x2, starting transfers between devices, shards(): lax.all_to_all(split_terms, 'shard', split_axis=1, concat_axis=1, tiled=T...  27.4 us
    dot_general x4, matrix products, expert_rows(): return jnp.dot(hidden, down_part, preferred_element_type=jnp.float32)  21.5 us
  transfers between devices with their start and end apart: 9, of which 9 were waited for; matrix products, arithmetic and copies ran while one was open for 0% of the time, Pallas kernels for 0%

commit v1 on v0

--- a/solution.py
+++ b/solution.py
@@ -4,6 +4,11 @@
 from jax.sharding import PartitionSpec as P
 
 FF = 16384
+
+
+def gather_by_exchange(array, axis, dim):
+    copies = jnp.concatenate([array] * lax.axis_size(axis), axis=dim)
+    return lax.all_to_all(copies, axis, dim, dim, tiled=True)
 
 
 def shifted(value, axis, steps):
@@ -46,7 +51,7 @@
     stored = jnp.zeros_like(tokens)
     for tick in range(segment_count):
         normed = normalize(carried, row_gain)
-        gathered = lax.all_gather(normed, "shard", axis=1, tiled=True)
+        gathered = gather_by_exchange(normed, "shard", 1)
         partial_sum = jnp.zeros(gathered.shape, jnp.float32)
 
         def add_block(block_id, acc):

time: 949 us -> 1040 us (1.096)
  waiting for transfers between devices: 532 us -> 439 us
  local copies, waits for them, and re-layouts: 76.8 us -> 160 us
  blocking collectives: 241 us -> 321 us
  starting transfers between devices: 36 us -> 62.8 us
  between operations: 14 us -> 1.1 us
    all_gather x4 -> x0, waiting for transfers between devices: 313 us -> none  [shards(): gathered = lax.all_gather(normed, 'shard', axis=1, tiled=True)]
    all_to_all x0 -> x3, waiting for transfers between devices: none -> 220 us  [gather_by_exchange(): return lax.all_to_all(copies, axis, dim, dim, tiled=True)]
    concatenate x0 -> x8, local copies, waits for them, and re-layouts: none -> 89.5 us  [gather_by_exchange(): copies = jnp.concatenate([array] * lax.axis_size(axis), axis=dim)]
    all_to_all x0 -> x1, blocking collectives: none -> 80.7 us  [gather_by_exchange(): return lax.all_to_all(copies, axis, dim, dim, tiled=True)]
    all_to_all x0 -> x3, starting transfers between devices: none -> 27.1 us  [gather_by_exchange(): return lax.all_to_all(copies, axis, dim, dim, tiled=True)]
  transfers between devices with their start and end apart: 9 -> 8, of which waited for: 9 -> 8; matrix products, arithmetic and copies ran while one was open for 0% -> 0% of each run, Pallas kernels for 0% -> 0%
where the time goes in v1:
time: 1040 us; the launch traced here: 1030 us
  waiting for transfers between devices  439 us (42%)
  blocking collectives  321 us (31%)
  local copies, waits for them, and re-layouts  160 us (15%)
  starting transfers between devices  62.8 us (6%)
  matrix products  28.3 us (3%)
  other arithmetic  18.2 us (2%)
    all_to_all x2, blocking collectives, shards(): lax.all_to_all(split_terms, 'shard', split_axis=1, concat_axis=1, tiled=T...  241 us
    all_to_all x3, waiting for transfers between devices, gather_by_exchange(): return lax.all_to_all(copies, axis, dim, dim, tiled=True)  220 us
    all_to_all x2, waiting for transfers between devices, shards(): lax.all_to_all(split_terms, 'shard', split_axis=1, concat_axis=1, tiled=T...  214 us
    concatenate x8, local copies, waits for them, and re-layouts, gather_by_exchange(): copies = jnp.concatenate([array] * lax.axis_size(axis), axis=dim)  89.5 us
    all_to_all x1, blocking collectives, gather_by_exchange(): return lax.all_to_all(copies, axis, dim, dim, tiled=True)  80.7 us
    reshape x8, local copies, waits for them, and re-layouts, shards(): partial_sum.reshape(block_total, shard_count, local_rows, width)  46.5 us
    all_to_all x2, starting transfers between devices, shards(): lax.all_to_all(split_terms, 'shard', split_axis=1, concat_axis=1, tiled=T...  27.2 us
    all_to_all x3, starting transfers between devices, gather_by_exchange(): return lax.all_to_all(copies, axis, dim, dim, tiled=True)  27.1 us
  transfers between devices with their start and end apart: 8, of which 8 were waited for; matrix products, arithmetic and copies ran while one was open for 0% of the time, Pallas kernels for 0%

profile of v1, /device:TPU:5, one launch (start us, length us, event | category | flops | bytes accessed | tf_op | source)
XLA Modules:
  0.0 1031.8 jit_solution(8767574746925726564)
XLA Ops:
  1.8 4.9 concatenate.12
  6.7 3.7 copy.26
  10.4 12.3 %all-to-all-start = ((bf16[3,128,3072]{2,0,1:T(4,128)(2,1)}), bf16[3,128,3072]{2,0,1:T(4,128)(2,1)S(1)}, u32[]{:S(2)}, u32[]{:S(2)}) async-start(bf16[3,128,3072]{2,0,1:T(4,128)(2,1)} %copy.26), calls=%async_computation | async-start | bytes 6291456 | tf_op jit(solution)/shard_map/all_to_all | solution.py:11
  23.4 72.8 %all-to-all-done = bf16[3,128,3072]{2,0,1:T(4,128)(2,1)S(1)} async-done(((bf16[3,128,3072]{2,0,1:T(4,128)(2,1)}), bf16[3,128,3072]{2,0,1:T(4,128)(2,1)S(1)}, u32[]{:S(2)}, u32[]{:S(2)}) %all-to-all-start) | async-done | bytes 2359328 | tf_op jit(solution)/shard_map/all_to_all | solution.py:11
  98.6 2.7 broadcast.59.clone
  101.4 7.1 while.40
  103.1 5.4 fusion.139
  108.5 6.6 reshape.46
  115.1 6.1 copy.28
  121.2 13.8 %all-to-all-start.1 = ((f32[3,64,2,3072]{3,2,0,1:T(2,128)}), f32[3,64,2,3072]{3,2,0,1:T(2,128)}, u32[]{:S(2)}, u32[]{:S(2)}) async-start(f32[3,64,2,3072]{3,2,0,1:T(2,128)} %copy.28), calls=%async_computation.1 | async-start | bytes 9437184 | tf_op jit(solution)/shard_map/all_to_all | solution.py:64
  135.1 106.8 %all-to-all-done.1 = f32[3,64,2,3072]{3,2,0,1:T(2,128)} async-done(((f32[3,64,2,3072]{3,2,0,1:T(2,128)}), f32[3,64,2,3072]{3,2,0,1:T(2,128)}, u32[]{:S(2)}, u32[]{:S(2)}) %all-to-all-start.1) | async-done | bytes 4718624 | tf_op jit(solution)/shard_map/all_to_all | solution.py:64
  241.9 3.7 reduce_sum.73
  245.7 2.8 collective-permute-start
  250.6 22.1 %concatenate.13 = bf16[3,128,3072]{2,1,0:T(8,128)(2,1)} concatenate(bf16[3,2,3072]{2,1,0:T(2,128)(2,1)S(1)} %fusion.82, bf16[3,2,3072]{2,1,0:T(2,128)(2,1)S(1)} %fusion.82, bf16[3,2,3072]{2,1,0:T(2,128)(2,1)S(1)} %fusion.82, bf16[3,2,3072]{2,1,0:T(2,128)(2,1)S(1)} %fusion.82, bf16[3,2,3072]{2,1,0:T(2,128)(2,1)S(1)} %fusion.82, bf16[3,2,3072]{2,1,0:T(2,128)(2,1)S(1)} %fusion.82, ...), dimensions={1} | concatenate | bytes 4718592 | tf_op jit(solution)/shard_map/concatenate | solution.py:10
  272.8 5.4 copy.29
  278.2 7.2 all-to-all-start.2
  285.3 73.4 %all-to-all-done.2 = bf16[3,128,3072]{2,0,1:T(4,128)(2,1)} async-done(((bf16[3,128,3072]{2,0,1:T(4,128)(2,1)}), bf16[3,128,3072]{2,0,1:T(4,128)(2,1)}, u32[]{:S(2)}, u32[]{:S(2)}) %all-to-all-start.2) | async-done | bytes 2359328 | tf_op jit(solution)/shard_map/all_to_all | solution.py:11
  358.8 4.2 copy.30
  363.0 2.7 broadcast.59.clone.1
  365.7 7.1 while.41
  367.4 5.4 fusion.146
  372.8 6.6 reshape.47
  379.4 4.0 copy.31
  383.3 120.5 %all_to_all.41 = f32[3,64,2,3072]{3,2,0,1:T(2,128)} all-to-all(f32[3,64,2,3072]{3,2,0,1:T(2,128)S(1)} %copy.31), channel_id=1, replica_groups=mesh['segment'=4,'shard'=64] {'shard'}, dimensions={1} | all-to-all | bytes 9437184 | tf_op jit(solution)/shard_map/all_to_all | solution.py:64
  503.8 3.7 reduce_sum.75
  507.6 2.8 collective-permute-start.1
  512.5 22.1 %concatenate.14 = bf16[3,128,3072]{2,1,0:T(8,128)(2,1)} concatenate(bf16[3,2,3072]{2,1,0:T(2,128)(2,1)S(1)} %fusion.86, bf16[3,2,3072]{2,1,0:T(2,128)(2,1)S(1)} %fusion.86, bf16[3,2,3072]{2,1,0:T(2,128)(2,1)S(1)} %fusion.86, bf16[3,2,3072]{2,1,0:T(2,128)(2,1)S(1)} %fusion.86, bf16[3,2,3072]{2,1,0:T(2,128)(2,1)S(1)} %fusion.86, bf16[3,2,3072]{2,1,0:T(2,128)(2,1)S(1)} %fusion.86, ...), dimensions={1} | concatenate | bytes 4718592 | tf_op jit(solution)/shard_map/concatenate | solution.py:10
  534.7 5.4 copy.32
  540.1 7.6 all-to-all-start.4
  547.7 73.4 %all-to-all-done.4 = bf16[3,128,3072]{2,0,1:T(4,128)(2,1)} async-done(((bf16[3,128,3072]{2,0,1:T(4,128)(2,1)}), bf16[3,128,3072]{2,0,1:T(4,128)(2,1)}, u32[]{:S(2)}, u32[]{:S(2)}) %all-to-all-start.4) | async-done | bytes 2359328 | tf_op jit(solution)/shard_map/all_to_all | solution.py:11
  621.1 4.2 copy.33
  628.0 7.5 while.42
  629.7 5.4 fusion.153
  635.5 6.6 reshape.48
  642.1 4.0 copy.34
  646.1 120.3 %all_to_all.42 = f32[3,64,2,3072]{3,2,0,1:T(2,128)} all-to-all(f32[3,64,2,3072]{3,2,0,1:T(2,128)S(1)} %copy.34), channel_id=1, replica_groups=mesh['segment'=4,'shard'=64] {'shard'}, dimensions={1} | all-to-all | bytes 9437184 | tf_op jit(solution)/shard_map/all_to_all | solution.py:64
  766.3 3.7 reduce_sum.77
  770.1 2.8 collective-permute-start.2
  775.1 22.1 %concatenate.15 = bf16[3,128,3072]{2,1,0:T(8,128)(2,1)} concatenate(bf16[3,2,3072]{2,1,0:T(2,128)(2,1)S(1)} %fusion.90, bf16[3,2,3072]{2,1,0:T(2,128)(2,1)S(1)} %fusion.90, bf16[3,2,3072]{2,1,0:T(2,128)(2,1)S(1)} %fusion.90, bf16[3,2,3072]{2,1,0:T(2,128)(2,1)S(1)} %fusion.90, bf16[3,2,3072]{2,1,0:T(2,128)(2,1)S(1)} %fusion.90, bf16[3,2,3072]{2,1,0:T(2,128)(2,1)S(1)} %fusion.90, ...), dimensions={1} | concatenate | bytes 4718592 | tf_op jit(solution)/shard_map/concatenate | solution.py:10
  797.2 3.7 copy.35
  800.9 80.7 %all_to_all.40 = bf16[3,128,3072]{2,0,1:T(4,128)(2,1)S(1)} all-to-all(bf16[3,128,3072]{2,0,1:T(4,128)(2,1)S(1)} %copy.35), channel_id=1, replica_groups=mesh['segment'=4,'shard'=64] {'shard'}, dimensions={1} | all-to-all | bytes 4718592 | tf_op jit(solution)/shard_map/all_to_all | solution.py:11
  886.7 7.3 while.43
  888.5 5.4 fusion.160
  893.9 6.6 reshape.49
  900.5 6.1 copy.37
  906.6 13.4 %all-to-all-start.7 = ((f32[3,64,2,3072]{3,2,0,1:T(2,128)}), f32[3,64,2,3072]{3,2,0,1:T(2,128)}, u32[]{:S(2)}, u32[]{:S(2)}) async-start(f32[3,64,2,3072]{3,2,0,1:T(2,128)} %copy.37), calls=%async_computation.7 | async-start | bytes 9437184 | tf_op jit(solution)/shard_map/all_to_all | solution.py:64
  920.0 107.1 %all-to-all-done.7 = f32[3,64,2,3072]{3,2,0,1:T(2,128)} async-done(((f32[3,64,2,3072]{3,2,0,1:T(2,128)}), f32[3,64,2,3072]{3,2,0,1:T(2,128)}, u32[]{:S(2)}, u32[]{:S(2)}) %all-to-all-start.7) | async-done | bytes 4718624 | tf_op jit(solution)/shard_map/all_to_all | solution.py:64
  1027.2 3.7 reduce_sum.79
  (40 shorter events, 26.3 us)
Async XLA Ops:
  10.4 85.8 %all-to-all-start = ((bf16[3,128,3072]{2,0,1:T(4,128)(2,1)}), bf16[3,128,3072]{2,0,1:T(4,128)(2,1)S(1)}, u32[]{:S(2)}, u32[]{:S(2)}) async-start(bf16[3,128,3072]{2,0,1:T(4,128)(2,1)} %copy.26), calls=%async_computation | async-start | bytes 6291456 | tf_op jit(solution)/shard_map/all_to_all | solution.py:11
  98.6 2.8 copy-start
  121.2 13.8 %copy-start.5 = (f32[1,3,2]{1,2,0:T(2,128)S(1)}, f32[1,3,2]{1,2,0:T(2,128)}, u32[]{:S(2)}) copy-start(f32[1,3,2]{1,2,0:T(2,128)} %param.21) | copy-start | bytes 76
  121.2 120.7 %all-to-all-start.1 = ((f32[3,64,2,3072]{3,2,0,1:T(2,128)}), f32[3,64,2,3072]{3,2,0,1:T(2,128)}, u32[]{:S(2)}, u32[]{:S(2)}) async-start(f32[3,64,2,3072]{3,2,0,1:T(2,128)} %copy.28), calls=%async_computation.1 | async-start | bytes 9437184 | tf_op jit(solution)/shard_map/all_to_all | solution.py:64
  134.9 110.6 %copy-start.1 = (bf16[3,2,3072]{2,1,0:T(2,128)(2,1)S(1)}, bf16[3,2,3072]{2,1,0:T(2,128)(2,1)}, u32[]{:S(2)}) copy-start(bf16[3,2,3072]{2,1,0:T(2,128)(2,1)} %param.15) | copy-start | bytes 110596
  135.0 115.6 %copy-start.2 = (f32[1,3072]{1,0:T(1,128)S(1)}, f32[1,3072]{1,0:T(1,128)}, u32[]{:S(2)}) copy-start(f32[1,3072]{1,0:T(1,128)} %param.16) | copy-start | bytes 36868
  245.7 4.7 collective-permute-start
  278.2 80.6 %all-to-all-start.2 = ((bf16[3,128,3072]{2,0,1:T(4,128)(2,1)}), bf16[3,128,3072]{2,0,1:T(4,128)(2,1)}, u32[]{:S(2)}, u32[]{:S(2)}) async-start(bf16[3,128,3072]{2,0,1:T(4,128)(2,1)} %copy.29), calls=%async_computation.2 | async-start | bytes 6291456 | tf_op jit(solution)/shard_map/all_to_all | solution.py:11
  507.6 4.7 collective-permute-start.1
  540.1 81.0 %all-to-all-start.4 = ((bf16[3,128,3072]{2,0,1:T(4,128)(2,1)}), bf16[3,128,3072]{2,0,1:T(4,128)(2,1)}, u32[]{:S(2)}, u32[]{:S(2)}) async-start(bf16[3,128,3072]{2,0,1:T(4,128)(2,1)} %copy.32), calls=%async_computation.4 | async-start | bytes 6291456 | tf_op jit(solution)/shard_map/all_to_all | solution.py:11
  770.1 30.8 %copy-start.3 = (bf16[3,2,3072]{2,1,0:T(2,128)(2,1)}, bf16[3,2,3072]{2,1,0:T(2,128)(2,1)S(1)}, u32[]{:S(2)}) copy-start(bf16[3,2,3072]{2,1,0:T(2,128)(2,1)S(1)} %fusion.87) | copy-start | bytes 110596
  770.1 4.7 collective-permute-start.2
  906.6 120.6 %all-to-all-start.7 = ((f32[3,64,2,3072]{3,2,0,1:T(2,128)}), f32[3,64,2,3072]{3,2,0,1:T(2,128)}, u32[]{:S(2)}, u32[]{:S(2)}) async-start(f32[3,64,2,3072]{3,2,0,1:T(2,128)} %copy.37), calls=%async_computation.7 | async-start | bytes 9437184 | tf_op jit(solution)/shard_map/all_to_all | solution.py:64
  920.0 110.8 %copy-start.4 = (bf16[3,2,3072]{2,1,0:T(2,128)(2,1)S(1)}, bf16[3,2,3072]{2,1,0:T(2,128)(2,1)}, u32[]{:S(2)}) copy-start(bf16[3,2,3072]{2,1,0:T(2,128)(2,1)} %copy-done.3) | copy-start | bytes 110596
